TPU v7x, 32 devices: a whole 2x2x4 slice. The times are simulated.
32 devices in a mesh: cols: 4 (over y, x), rows: 8 (over z, core).
Axes of the slice: x: 2, y: 2, z: 4, core: 2. Of those that a mesh axis runs over, the one named last changes fastest.
Arguments:
- gradient: float32 [128, 8192], P('cols', 'rows'), may hold values from -100 to 100
- width_factor: float32 [128, 128], P(None, 'cols'), may hold values from -3 to 4, as said below
- diag_blocks: float32 [64, 128, 128], P('rows'), may hold values from -2 to 24, as said below
- jacobi_inverse: float32 [64, 128, 128], P('rows'), may hold values from -2 to 2, as said below
- coupling_tiles: bfloat16 [32, 128, 128], P('rows'), may hold values from -4 to 4, as said below
- tile_local: int32 [32], P('rows'), may hold values from 0 to 7
- tile_remote: int32 [32], P('rows'), may hold values from 0 to 63, as said below
- tile_count: int32 [8], P('rows'), may hold values from 0 to 3, as said below
Outputs:
- solution: float32 [128, 8192], P('cols', 'rows')
- residual: float32 [128, 8192], P('cols', 'rows')
Inputs may be any that keep to these rules, and one draw needn't show every extreme that they name: `tile_remote`: the live entries are the first tile_count entries of each device's list; they name distinct devices other than the owner, each at most once. For a live entry of device d naming block J of device e, device e has a live entry naming d's block with its tile the transpose. Pad entries hold valid indices. `tile_count`: at most 3 on one device, reached on some device. `coupling_tiles`: with diag_blocks and the live entries, M is symmetric positive definite. `diag_blocks`: symmetric positive definite tiles. `jacobi_inverse`: the inverses of diag_blocks, symmetric. `width_factor`: symmetric positive definite.
All inputs are finite; a program needn't handle non-finite values.
Results may differ from a plain program's by a relative error of at most 0.0085.
Values may be sent and summed in bfloat16 or wider, within the bound.
No kernel may reach another device: no remote copies, remote signals or barrier semaphores. Data moves between devices by JAX's collectives and lax.ppermute only.
A program may use at most 64 MiB of HBM per device.

v0:
```python
import jax
import jax.numpy as jnp
from jax import lax
from jax.sharding import PartitionSpec as P

BLOCK = 128
ITERS = 6
highest = lax.Precision.HIGHEST


def on_device(
    gradient,
    width_factor,
    diag_blocks,
    jacobi_inverse,
    coupling_tiles,
    tile_local,
    tile_remote,
    tile_count,
):
    width_dev, rows_dev = gradient.shape
    blocks_dev = diag_blocks.shape[0]
    slot_count = tile_local.shape[0]
    devices = lax.axis_size("rows")
    active_slot = jnp.arange(slot_count, dtype=jnp.int32) < tile_count[0]
    placing = (
        (tile_local[:, None] == jnp.arange(blocks_dev, dtype=jnp.int32)[None, :])
        & active_slot[:, None]
    ).astype(jnp.float32)
    owner_dev = tile_remote // blocks_dev
    matches = active_slot[:, None] & (
        owner_dev[:, None] == jnp.arange(devices, dtype=jnp.int32)[None, :]
    )
    request = jnp.sum(jnp.where(matches, (tile_remote % blocks_dev)[:, None], 0), axis=0)
    granted = lax.all_to_all(request, "rows", split_axis=0, concat_axis=0, tiled=True)

    def precondition(vector):
        blocks = vector.reshape(width_dev, blocks_dev, BLOCK)
        return jnp.einsum("enj,nji->eni", blocks, jacobi_inverse, precision=highest).reshape(
            width_dev, rows_dev
        )

    solution = jnp.zeros_like(gradient)
    residual = gradient
    precond_res = precondition(residual)
    direction = precond_res
    res_norm = lax.psum(jnp.sum(residual * precond_res), ("cols", "rows"))
    for iteration in range(ITERS):
        apply_blocks = direction.reshape(width_dev, blocks_dev, BLOCK)
        local_part = jnp.einsum("enj,nji->eni", apply_blocks, diag_blocks, precision=highest)
        rounded = direction.astype(jnp.bfloat16).reshape(width_dev, blocks_dev, BLOCK)
        incoming = lax.all_to_all(
            rounded[:, granted, :], "rows", split_axis=1, concat_axis=1, tiled=True
        )
        sources = incoming[:, owner_dev, :]
        products = jnp.einsum(
            "ekj,kji->eki", sources, coupling_tiles, preferred_element_type=jnp.float32
        )
        coupled = jnp.einsum("eki,kb->ebi", products, placing, precision=highest)
        summed = lax.psum(
            jnp.dot(
                width_factor, (local_part + coupled).reshape(width_dev, rows_dev), precision=highest
            ),
            "cols",
        )
        fisher_dir = lax.dynamic_slice_in_dim(
            summed, lax.axis_index("cols") * width_dev, width_dev, 0
        )
        precond_fisher = precondition(fisher_dir)
        curvature, cross_term, second_term = lax.psum(
            (
                jnp.sum(direction * fisher_dir),
                jnp.sum(fisher_dir * precond_res),
                jnp.sum(fisher_dir * precond_fisher),
            ),
            ("cols", "rows"),
        )
        step_size = res_norm / curvature
        solution = solution + step_size * direction
        residual = residual - step_size * fisher_dir
        if iteration + 1 < ITERS:
            precond_res = precond_res - step_size * precond_fisher
            next_norm = (
                res_norm - 2.0 * step_size * cross_term + step_size * step_size * second_term
            )
            direction = precond_res + next_norm / res_norm * direction
            res_norm = next_norm
    return (solution, residual)


def solution(mesh):
    placed = (
        P("cols", "rows"),
        P(None, "cols"),
        P("rows", None, None),
        P("rows", None, None),
        P("rows", None, None),
        P("rows"),
        P("rows"),
        P("rows"),
    )
    return jax.shard_map(
        on_device,
        mesh=mesh,
        in_specs=placed,
        out_specs=(P("cols", "rows"), P("cols", "rows")),
        check_vma=False,
    )
```

profile of v0, /device:TPU:0, one launch (start us, length us, event | category | flops | bytes accessed | tf_op | source)
XLA Modules:
  0.0 644.4 jit_solution(5383939424549361704)
XLA Ops:
  7.9 0.6 copy-done.6
  8.6 0.7 copy.175
  9.3 6.4 all-to-all-start
  15.7 1.5 bitcast_convert_fusion
  17.2 4.0 all-to-all-done
  21.4 1.2 gather_fusion
  22.6 3.4 all-to-all-start.1
  26.1 5.7 all-to-all-done.1
  33.6 1.4 convolution_bitcast_fusion.5
  35.1 44.0 %all-reduce.12.cloned.1.call-done = f32[128,1024]{1,0:T(8,128)} async-done(((f32[128,1024]{1,0:T(8,128)}), f32[128,1024]{1,0:T(8,128)}) %all-reduce.12.cloned.1.call-update) | async-done | bytes 524304 | tf_op jit(solution)/shard_map/psum | solution.py:60
  79.0 1.5 fusion.49
  80.5 1.6 fusion.25
  82.1 39.6 %all-reduce.4 = (f32[]{:T(128)}, f32[]{:T(128)}, f32[]{:T(128)}) all-reduce(f32[]{:T(128)} %get-tuple-element.24, f32[]{:T(128)} %get-tuple-element.23, f32[]{:T(128)} %get-tuple-element.22), channel_id=1, replica_groups=mesh['cols'=4,'rows'=8] {'cols','rows'}, use_global_device_ids=true, to_apply=%region_1.2 | all-reduce | flops 3 | bytes 24 | tf_op jit(solution)/shard_map/psum | solution.py:47
  125.5 0.6 gather_fusion.2
  126.0 9.3 %all_to_all.42 = bf16[32,8,128]{2,0,1:T(8,128)(2,1)S(1)} all-to-all(bf16[32,8,128]{2,0,1:T(8,128)(2,1)S(1)} %bitcast.343), channel_id=1, replica_groups=mesh['cols'=4,'rows'=8] {'rows'}, dimensions={1} | all-to-all | bytes 131072 | tf_op jit(solution)/shard_map/all_to_all | solution.py:52
  136.9 1.4 convolution_bitcast_fusion.4
  138.4 45.0 %all-reduce.14.cloned.1.call-done = f32[128,1024]{1,0:T(8,128)} async-done(((f32[128,1024]{1,0:T(8,128)}), f32[128,1024]{1,0:T(8,128)}) %all-reduce.14.cloned.1.call-update) | async-done | bytes 524304 | tf_op jit(solution)/shard_map/psum | solution.py:60
  183.4 1.5 fusion.46
  184.9 0.8 fusion.21
  185.7 39.6 %all-reduce.3 = (f32[]{:T(128)}, f32[]{:T(128)}, f32[]{:T(128)}) all-reduce(f32[]{:T(128)} %get-tuple-element.21, f32[]{:T(128)} %get-tuple-element.20, f32[]{:T(128)} %get-tuple-element.19), channel_id=1, replica_groups=mesh['cols'=4,'rows'=8] {'cols','rows'}, use_global_device_ids=true, to_apply=%region_10.11 | all-reduce | flops 3 | bytes 24 | tf_op jit(solution)/shard_map/psum | solution.py:70
  227.3 0.6 gather_fusion.4
  227.8 9.3 %all_to_all.43 = bf16[32,8,128]{2,0,1:T(8,128)(2,1)S(1)} all-to-all(bf16[32,8,128]{2,0,1:T(8,128)(2,1)S(1)} %bitcast.344), channel_id=1, replica_groups=mesh['cols'=4,'rows'=8] {'rows'}, dimensions={1} | all-to-all | bytes 131072 | tf_op jit(solution)/shard_map/all_to_all | solution.py:52
  238.6 1.4 convolution_bitcast_fusion.3
  240.2 45.0 %all-reduce.16.cloned.1.call-done = f32[128,1024]{1,0:T(8,128)} async-done(((f32[128,1024]{1,0:T(8,128)}), f32[128,1024]{1,0:T(8,128)}) %all-reduce.16.cloned.1.call-update) | async-done | bytes 524304 | tf_op jit(solution)/shard_map/psum | solution.py:60
  285.2 1.5 fusion.43
  286.6 1.7 multiply_reduce_fusion.5
  288.3 39.6 %all-reduce.2 = (f32[]{:T(128)}, f32[]{:T(128)}, f32[]{:T(128)}) all-reduce(f32[]{:T(128)} %get-tuple-element.13, f32[]{:T(128)} %get-tuple-element.12, f32[]{:T(128)} %get-tuple-element.18), channel_id=1, replica_groups=mesh['cols'=4,'rows'=8] {'cols','rows'}, use_global_device_ids=true, to_apply=%region_17.18 | all-reduce | flops 3 | bytes 24 | tf_op jit(solution)/shard_map/psum | solution.py:70
  329.9 0.6 gather_fusion.6
  330.4 9.3 %all_to_all.44 = bf16[32,8,128]{2,0,1:T(8,128)(2,1)S(1)} all-to-all(bf16[32,8,128]{2,0,1:T(8,128)(2,1)S(1)} %bitcast.345), channel_id=1, replica_groups=mesh['cols'=4,'rows'=8] {'rows'}, dimensions={1} | all-to-all | bytes 131072 | tf_op jit(solution)/shard_map/all_to_all | solution.py:52
  341.3 1.4 convolution_bitcast_fusion.2
  342.8 45.0 %all-reduce.18.cloned.1.call-done = f32[128,1024]{1,0:T(8,128)} async-done(((f32[128,1024]{1,0:T(8,128)}), f32[128,1024]{1,0:T(8,128)}) %all-reduce.18.cloned.1.call-update) | async-done | bytes 524304 | tf_op jit(solution)/shard_map/psum | solution.py:60
  387.8 1.5 fusion.40
  389.2 1.6 fusion.13
  390.8 39.7 %all-reduce.1 = (f32[]{:T(128)}, f32[]{:T(128)}, f32[]{:T(128)}) all-reduce(f32[]{:T(128)} %get-tuple-element.17, f32[]{:T(128)} %get-tuple-element.16, f32[]{:T(128)} %get-tuple-element.15), channel_id=1, replica_groups=mesh['cols'=4,'rows'=8] {'cols','rows'}, use_global_device_ids=true, to_apply=%region_24.25 | all-reduce | flops 3 | bytes 24 | tf_op jit(solution)/shard_map/psum | solution.py:70
  433.2 9.3 %all_to_all.45 = bf16[32,8,128]{2,0,1:T(8,128)(2,1)S(1)} all-to-all(bf16[32,8,128]{2,0,1:T(8,128)(2,1)S(1)} %bitcast.346), channel_id=1, replica_groups=mesh['cols'=4,'rows'=8] {'rows'}, dimensions={1} | all-to-all | bytes 131072 | tf_op jit(solution)/shard_map/all_to_all | solution.py:52
  443.5 0.6 fusion.1
  444.0 1.4 convolution_bitcast_fusion.1
  445.5 45.1 %all-reduce.20.cloned.1.call-done = f32[128,1024]{1,0:T(8,128)} async-done(((f32[128,1024]{1,0:T(8,128)}), f32[128,1024]{1,0:T(8,128)}) %all-reduce.20.cloned.1.call-update) | async-done | bytes 524304 | tf_op jit(solution)/shard_map/psum | solution.py:60
  490.6 1.5 fusion.37
  492.1 1.6 multiply_reduce_fusion.1
  493.6 39.6 %all-reduce = (f32[]{:T(128)}, f32[]{:T(128)}, f32[]{:T(128)}) all-reduce(f32[]{:T(128)} %get-tuple-element.11, f32[]{:T(128)} %get-tuple-element.10, f32[]{:T(128)} %get-tuple-element.14), channel_id=1, replica_groups=mesh['cols'=4,'rows'=8] {'cols','rows'}, use_global_device_ids=true, to_apply=%region_31.32 | all-reduce | flops 3 | bytes 24 | tf_op jit(solution)/shard_map/psum | solution.py:70
  535.8 9.3 %all_to_all.46 = bf16[32,8,128]{2,0,1:T(8,128)(2,1)S(1)} all-to-all(bf16[32,8,128]{2,0,1:T(8,128)(2,1)S(1)} %bitcast.342), channel_id=1, replica_groups=mesh['cols'=4,'rows'=8] {'rows'}, dimensions={1} | all-to-all | bytes 131072 | tf_op jit(solution)/shard_map/all_to_all | solution.py:52
  546.6 1.4 convolution_bitcast_fusion
  548.1 45.1 %all-reduce.22.cloned.1.call-done = f32[128,1024]{1,0:T(8,128)} async-done(((f32[128,1024]{1,0:T(8,128)}), f32[128,1024]{1,0:T(8,128)}) %all-reduce.22.cloned.1.call-update) | async-done | bytes 524304 | tf_op jit(solution)/shard_map/psum | solution.py:60
  593.2 1.5 multiply_reduce_fusion
  594.7 39.5 %psum.178 = f32[]{:T(128)} all-reduce(f32[]{:T(128)} %multiply_reduce_fusion), channel_id=1, replica_groups=mesh['cols'=4,'rows'=8] {'cols','rows'}, use_global_device_ids=true, to_apply=%region_38.39 | all-reduce | flops 1 | bytes 8 | tf_op jit(solution)/shard_map/psum | solution.py:70
  634.9 0.7 fusion.35
  635.7 1.9 multiply_subtract_fusion
  (65 shorter events, 10.9 us)
Async XLA Ops:
  7.2 8.5 %copy-start = (f32[8,128,128]{2,1,0:T(8,128)S(1)}, f32[8,128,128]{2,1,0:T(8,128)}, u32[]{:S(2)}) copy-start(f32[8,128,128]{2,1,0:T(8,128)} %param.11) | copy-start | bytes 1572868
  7.9 0.7 copy-start.6
  9.3 11.9 %all-to-all-start = ((s32[8,1,1]{2,1,0:T(1,128)}), s32[8,1,1]{2,1,0:T(1,128)S(1)}, u32[]{:S(2)}, u32[]{:S(2)}) async-start(s32[8,1,1]{2,1,0:T(1,128)} %copy.175), calls=%async_computation | async-start | bytes 8192 | tf_op jit(solution)/shard_map/all_to_all | solution.py:35
  15.7 10.4 %copy-start.7 = (s32[4]{0:T(128)S(1)}, s32[4]{0:T(128)}, u32[]{:S(2)}) copy-start(s32[4]{0:T(128)} %param.13) | copy-start | bytes 52
  15.7 16.7 %copy-start.2 = (bf16[4,128,128]{2,1,0:T(8,128)(2,1)S(1)}, bf16[4,128,128]{2,1,0:T(8,128)(2,1)}, u32[]{:S(2)}) copy-start(bf16[4,128,128]{2,1,0:T(8,128)(2,1)} %param.12) | copy-start | bytes 393220
  17.2 15.6 %copy-start.1 = (f32[8,128,128]{2,1,0:T(8,128)S(1)}, f32[8,128,128]{2,1,0:T(8,128)}, u32[]{:S(2)}) copy-start(f32[8,128,128]{2,1,0:T(8,128)} %param.10) | copy-start | bytes 1572868
  22.6 9.2 %all-to-all-start.1 = ((bf16[32,8,128]{2,0,1:T(8,128)(2,1)}), bf16[32,8,128]{2,0,1:T(8,128)(2,1)S(1)}, u32[]{:S(2)}, u32[]{:S(2)}) async-start(bf16[32,8,128]{2,0,1:T(8,128)(2,1)} %bitcast.5), calls=%async_computation.1 | async-start | bytes 131072 | tf_op jit(solution)/shard_map/all_to_all | solution.py:52
  26.0 53.0 %all-reduce.12.cloned.1.call-start = ((), (), s32[]{:S(2)}) async-start(), calls=%async_computation.7 | async-start | bytes 1048576 | tf_op jit(solution)/shard_map/psum | solution.py:60
  32.8 0.7 copy-start.4
  35.0 148.4 %all-reduce.14.cloned.1.call-start = ((), (), s32[]{:S(2)}) async-start(), calls=%async_computation.8 | async-start | bytes 1048576 | tf_op jit(solution)/shard_map/psum | solution.py:60
  35.1 45.4 %copy-start.3 = (f32[32,1024]{1,0:T(8,128)S(1)}, f32[32,1024]{1,0:T(8,128)}, u32[]{:S(2)}) copy-start(f32[32,1024]{1,0:T(8,128)} %param.8) | copy-start | bytes 393220
  138.3 146.9 %all-reduce.16.cloned.1.call-start = ((), (), s32[]{:S(2)}) async-start(), calls=%async_computation.9 | async-start | bytes 1048576 | tf_op jit(solution)/shard_map/psum | solution.py:60
  183.4 1.5 copy-start.5
  240.1 147.7 %all-reduce.18.cloned.1.call-start = ((), (), s32[]{:S(2)}) async-start(), calls=%async_computation.10 | async-start | bytes 1048576 | tf_op jit(solution)/shard_map/psum | solution.py:60
  342.7 147.9 %all-reduce.20.cloned.1.call-start = ((), (), s32[]{:S(2)}) async-start(), calls=%async_computation.11 | async-start | bytes 1048576 | tf_op jit(solution)/shard_map/psum | solution.py:60
  445.5 147.7 %all-reduce.22.cloned.1.call-start = ((), (), s32[]{:S(2)}) async-start(), calls=%async_computation.12 | async-start | bytes 1048576 | tf_op jit(solution)/shard_map/psum | solution.py:60
Sparse Core Ops, SparseCore 0:
  35.1 43.8 all-reduce.11
  138.4 44.9 all-reduce.13
  240.2 44.9 all-reduce.15
  342.8 44.8 all-reduce.17
  445.6 44.9 all-reduce.19
  548.2 44.9 all-reduce.21
where the time goes:
time: 646 us; the launch traced here: 644 us
  blocking collectives  284 us (44%)
  waiting for transfers between devices  279 us (43%)
  between operations  27.4 us (4%)
  matrix products  23.3 us (4%)
  other arithmetic  12 us (2%)
  starting transfers between devices  9.95 us (2%)
  local copies, waits for them, and re-layouts  8.86 us (1%)
    psum x6, waiting for transfers between devices, on_device(): lax.psum(jnp.dot(width_factor, (local_part + coupled).reshape(width_dev,...  269 us
    psum x5, blocking collectives, on_device(): lax.psum((jnp.sum(direction * fisher_dir), jnp.sum(fisher_dir * precond_r...  198 us
    all_to_all x5, blocking collectives, on_device(): lax.all_to_all(rounded[:, granted, :], 'rows', split_axis=1, concat_axis=...  46.4 us
    psum x1, blocking collectives, on_device(): res_norm = lax.psum(jnp.sum(residual * precond_res), ('cols', 'rows'))  39.6 us
  transfers between devices with their start and end apart: 8, of which 8 were waited for; matrix products, arithmetic and copies ran while one was open for 0% of the time, Pallas kernels for 0%

commit v1 on v0

--- a/solution.py
+++ b/solution.py
@@ -6,6 +6,10 @@
 BLOCK = 128
 ITERS = 6
 highest = lax.Precision.HIGHEST
+
+
+def recast_the_loops(x_local, link_axis):
+    return jnp.sum(lax.all_gather(x_local, axis_name=link_axis), 0)
 
 
 def on_device(
@@ -57,11 +61,11 @@
             "ekj,kji->eki", sources, coupling_tiles, preferred_element_type=jnp.float32
         )
         coupled = jnp.einsum("eki,kb->ebi", products, placing, precision=highest)
-        summed = lax.psum(
+        summed = recast_the_loops(
             jnp.dot(
                 width_factor, (local_part + coupled).reshape(width_dev, rows_dev), precision=highest
             ),
-            "cols",
+            link_axis="cols",
         )
         fisher_dir = lax.dynamic_slice_in_dim(
             summed, lax.axis_index("cols") * width_dev, width_dev, 0

time: 646 us -> 615 us (0.952)
  waiting for transfers between devices: 279 us -> 217 us
  local copies, waits for them, and re-layouts: 8.86 us -> 28.8 us
  other arithmetic: 12 us -> 23.8 us
    psum x6 -> x0, waiting for transfers between devices: 269 us -> none  [on_device(): lax.psum(jnp.dot(width_factor, (local_part + coupled).reshape(width_dev,...]
    all_gather x0 -> x6, waiting for transfers between devices: none -> 207 us  [recast_the_loops(): return jnp.sum(lax.all_gather(x_local, axis_name=link_axis), 0)]
    reduce_sum x0 -> x6, other arithmetic: none -> 11.9 us  [recast_the_loops(): return jnp.sum(lax.all_gather(x_local, axis_name=link_axis), 0)]
    all_gather x0 -> x6, local copies, waits for them, and re-layouts: none -> 11.6 us  [recast_the_loops(): return jnp.sum(lax.all_gather(x_local, axis_name=link_axis), 0)]
    dynamic_slice x0 -> x6, local copies, waits for them, and re-layouts: none -> 6.7 us  [on_device(): lax.dynamic_slice_in_dim(summed, lax.axis_index('cols') * width_dev, widt...]
where the time goes in v1:
time: 615 us; the launch traced here: 613 us
  blocking collectives  284 us (46%)
  waiting for transfers between devices  217 us (35%)
  local copies, waits for them, and re-layouts  28.8 us (5%)
  between operations  27.7 us (5%)
  other arithmetic  23.8 us (4%)
  matrix products  22.8 us (4%)
  starting transfers between devices  9.95 us (2%)
    all_gather x6, waiting for transfers between devices, recast_the_loops(): return jnp.sum(lax.all_gather(x_local, axis_name=link_axis), 0)  207 us
    psum x5, blocking collectives, on_device(): lax.psum((jnp.sum(direction * fisher_dir), jnp.sum(fisher_dir * precond_r...  198 us
    all_to_all x5, blocking collectives, on_device(): lax.all_to_all(rounded[:, granted, :], 'rows', split_axis=1, concat_axis=...  46.4 us
    psum x1, blocking collectives, on_device(): res_norm = lax.psum(jnp.sum(residual * precond_res), ('cols', 'rows'))  39.6 us
  transfers between devices with their start and end apart: 8, of which 8 were waited for; matrix products, arithmetic and copies ran while one was open for 0% of the time, Pallas kernels for 0%

profile of v1, /device:TPU:0, one launch (start us, length us, event | category | flops | bytes accessed | tf_op | source)
XLA Modules:
  0.0 613.1 jit_solution(1040607999040789251)
XLA Ops:
  9.3 6.4 %all-to-all-start = ((s32[8,1,1]{2,1,0:T(1,128)}), s32[8,1,1]{2,1,0:T(1,128)S(1)}, u32[]{:S(2)}, u32[]{:S(2)}) async-start(s32[8,1,1]{2,1,0:T(1,128)} %copy.149), calls=%async_computation | async-start | bytes 8192 | tf_op jit(solution)/shard_map/all_to_all | solution.py:39
  15.7 1.5 bitcast_convert_fusion
  17.2 4.0 all-to-all-done
  22.7 3.4 all-to-all-start.1
  26.8 5.0 all-to-all-done.1
  33.8 1.6 fusion.5
  35.4 1.8 convolution_bitcast_fusion.5
  37.2 33.6 %all-gather.13.cloned.1.call-done = f32[512,1024]{0,1:T(8,128)} async-done(((f32[128,1024]{0,1:T(8,128)}), f32[512,1024]{0,1:T(8,128)}) %all-gather.13.cloned.1.call-update) | async-done | bytes 2097168 | tf_op jit(solution)/shard_map/all_gather | solution.py:12
  70.9 1.9 reshape.220
  75.8 39.6 %all-reduce.4 = (f32[]{:T(128)}, f32[]{:T(128)}, f32[]{:T(128)}) all-reduce(f32[]{:T(128)} %get-tuple-element.20, f32[]{:T(128)} %get-tuple-element.19, f32[]{:T(128)} %get-tuple-element.18), channel_id=1, replica_groups=mesh['cols'=4,'rows'=8] {'cols','rows'}, use_global_device_ids=true, to_apply=%region_1.2 | all-reduce | flops 3 | bytes 24 | tf_op jit(solution)/shard_map/psum | solution.py:51
  119.8 9.3 %all_to_all.42 = bf16[32,8,128]{2,0,1:T(8,128)(2,1)S(1)} all-to-all(bf16[32,8,128]{2,0,1:T(8,128)(2,1)S(1)} %bitcast.355), channel_id=1, replica_groups=mesh['cols'=4,'rows'=8] {'rows'}, dimensions={1} | all-to-all | bytes 131072 | tf_op jit(solution)/shard_map/all_to_all | solution.py:56
  130.8 1.8 convolution_bitcast_fusion.4
  132.7 34.7 %all-gather.15.cloned.1.call-done = f32[512,1024]{0,1:T(8,128)} async-done(((f32[128,1024]{0,1:T(8,128)}), f32[512,1024]{0,1:T(8,128)}) %all-gather.15.cloned.1.call-update) | async-done | bytes 2097168 | tf_op jit(solution)/shard_map/all_gather | solution.py:12
  167.4 1.9 reshape.221
  169.3 2.1 reduce_sum.216
  173.5 1.4 fusion.21
  174.8 39.6 %all-reduce.3 = (f32[]{:T(128)}, f32[]{:T(128)}, f32[]{:T(128)}) all-reduce(f32[]{:T(128)} %get-tuple-element.17, f32[]{:T(128)} %get-tuple-element.16, f32[]{:T(128)} %get-tuple-element.15), channel_id=1, replica_groups=mesh['cols'=4,'rows'=8] {'cols','rows'}, use_global_device_ids=true, to_apply=%region_10.11 | all-reduce | flops 3 | bytes 24 | tf_op jit(solution)/shard_map/psum | solution.py:74
  217.7 9.3 %all_to_all.43 = bf16[32,8,128]{2,0,1:T(8,128)(2,1)S(1)} all-to-all(bf16[32,8,128]{2,0,1:T(8,128)(2,1)S(1)} %bitcast.356), channel_id=1, replica_groups=mesh['cols'=4,'rows'=8] {'rows'}, dimensions={1} | all-to-all | bytes 131072 | tf_op jit(solution)/shard_map/all_to_all | solution.py:56
  228.7 1.8 convolution_bitcast_fusion.3
  230.6 34.7 %all-gather.17.cloned.1.call-done = f32[512,1024]{0,1:T(8,128)} async-done(((f32[128,1024]{0,1:T(8,128)}), f32[512,1024]{0,1:T(8,128)}) %all-gather.17.cloned.1.call-update) | async-done | bytes 2097168 | tf_op jit(solution)/shard_map/all_gather | solution.py:12
  265.3 1.9 reshape.222
  267.2 2.1 reduce_sum.220
  269.4 1.3 constant_dynamic-slice_fusion.3
  271.4 1.4 multiply_reduce_fusion.5
  272.8 39.6 %all-reduce.2 = (f32[]{:T(128)}, f32[]{:T(128)}, f32[]{:T(128)}) all-reduce(f32[]{:T(128)} %get-tuple-element.9, f32[]{:T(128)} %get-tuple-element.8, f32[]{:T(128)} %get-tuple-element.14), channel_id=1, replica_groups=mesh['cols'=4,'rows'=8] {'cols','rows'}, use_global_device_ids=true, to_apply=%region_17.18 | all-reduce | flops 3 | bytes 24 | tf_op jit(solution)/shard_map/psum | solution.py:74
  315.1 9.3 %all_to_all.44 = bf16[32,8,128]{2,0,1:T(8,128)(2,1)S(1)} all-to-all(bf16[32,8,128]{2,0,1:T(8,128)(2,1)S(1)} %bitcast.357), channel_id=1, replica_groups=mesh['cols'=4,'rows'=8] {'rows'}, dimensions={1} | all-to-all | bytes 131072 | tf_op jit(solution)/shard_map/all_to_all | solution.py:56
  326.1 1.8 convolution_bitcast_fusion.2
  328.0 34.8 %all-gather.19.cloned.1.call-done = f32[512,1024]{0,1:T(8,128)} async-done(((f32[128,1024]{0,1:T(8,128)}), f32[512,1024]{0,1:T(8,128)}) %all-gather.19.cloned.1.call-update) | async-done | bytes 2097168 | tf_op jit(solution)/shard_map/all_gather | solution.py:12
  362.7 1.9 reshape.223
  364.7 2.1 reduce_sum.224
  366.8 1.3 constant_dynamic-slice_fusion.2
  368.9 1.4 fusion.13
  370.3 39.6 %all-reduce.1 = (f32[]{:T(128)}, f32[]{:T(128)}, f32[]{:T(128)}) all-reduce(f32[]{:T(128)} %get-tuple-element.13, f32[]{:T(128)} %get-tuple-element.12, f32[]{:T(128)} %get-tuple-element.11), channel_id=1, replica_groups=mesh['cols'=4,'rows'=8] {'cols','rows'}, use_global_device_ids=true, to_apply=%region_24.25 | all-reduce | flops 3 | bytes 24 | tf_op jit(solution)/shard_map/psum | solution.py:74
  412.6 9.3 %all_to_all.45 = bf16[32,8,128]{2,0,1:T(8,128)(2,1)S(1)} all-to-all(bf16[32,8,128]{2,0,1:T(8,128)(2,1)S(1)} %bitcast.358), channel_id=1, replica_groups=mesh['cols'=4,'rows'=8] {'rows'}, dimensions={1} | all-to-all | bytes 131072 | tf_op jit(solution)/shard_map/all_to_all | solution.py:56
  423.6 1.8 convolution_bitcast_fusion.1
  425.5 34.8 %all-gather.21.cloned.1.call-done = f32[512,1024]{0,1:T(8,128)} async-done(((f32[128,1024]{0,1:T(8,128)}), f32[512,1024]{0,1:T(8,128)}) %all-gather.21.cloned.1.call-update) | async-done | bytes 2097168 | tf_op jit(solution)/shard_map/all_gather | solution.py:12
  460.2 1.9 reshape.224
  462.2 2.1 reduce_sum.228
  464.3 1.3 constant_dynamic-slice_fusion.1
  467.7 39.5 %all-reduce = (f32[]{:T(128)}, f32[]{:T(128)}, f32[]{:T(128)}) all-reduce(f32[]{:T(128)} %get-tuple-element.7, f32[]{:T(128)} %get-tuple-element.6, f32[]{:T(128)} %get-tuple-element.10), channel_id=1, replica_groups=mesh['cols'=4,'rows'=8] {'cols','rows'}, use_global_device_ids=true, to_apply=%region_31.32 | all-reduce | flops 3 | bytes 24 | tf_op jit(solution)/shard_map/psum | solution.py:74
  509.9 9.3 %all_to_all.46 = bf16[32,8,128]{2,0,1:T(8,128)(2,1)S(1)} all-to-all(bf16[32,8,128]{2,0,1:T(8,128)(2,1)S(1)} %bitcast.354), channel_id=1, replica_groups=mesh['cols'=4,'rows'=8] {'rows'}, dimensions={1} | all-to-all | bytes 131072 | tf_op jit(solution)/shard_map/all_to_all | solution.py:56
  520.8 1.8 convolution_bitcast_fusion
  522.7 34.8 %all-gather.23.cloned.1.call-done = f32[512,1024]{0,1:T(8,128)} async-done(((f32[128,1024]{0,1:T(8,128)}), f32[512,1024]{0,1:T(8,128)}) %all-gather.23.cloned.1.call-update) | async-done | bytes 2097168 | tf_op jit(solution)/shard_map/all_gather | solution.py:12
  557.5 1.9 reshape.225
  559.4 2.1 reduce_sum.232
  561.6 1.3 constant_dynamic-slice_fusion
  563.1 1.6 multiply_reduce_fusion
  564.7 39.4 %psum.130 = f32[]{:T(128)} all-reduce(f32[]{:T(128)} %multiply_reduce_fusion), channel_id=1, replica_groups=mesh['cols'=4,'rows'=8] {'cols','rows'}, use_global_device_ids=true, to_apply=%region_38.39 | all-reduce | flops 1 | bytes 8 | tf_op jit(solution)/shard_map/psum | solution.py:74
  (167 shorter events, 28.6 us)
Async XLA Ops:
  7.2 8.5 %copy-start = (f32[8,128,128]{2,1,0:T(8,128)S(1)}, f32[8,128,128]{2,1,0:T(8,128)}, u32[]{:S(2)}) copy-start(f32[8,128,128]{2,1,0:T(8,128)} %param.11) | copy-start | bytes 1572868
  7.2 28.2 %copy-start.37 = (f32[128,32]{0,1:T(8,128)S(1)}, f32[128,32]{0,1:T(8,128)}, u32[]{:S(2)}) copy-start(f32[128,32]{0,1:T(8,128)} %param.9) | copy-start | bytes 49156
  9.3 11.9 %all-to-all-start = ((s32[8,1,1]{2,1,0:T(1,128)}), s32[8,1,1]{2,1,0:T(1,128)S(1)}, u32[]{:S(2)}, u32[]{:S(2)}) async-start(s32[8,1,1]{2,1,0:T(1,128)} %copy.149), calls=%async_computation | async-start | bytes 8192 | tf_op jit(solution)/shard_map/all_to_all | solution.py:39
  21.5 5.3 copy-start.45
  22.7 9.2 %all-to-all-start.1 = ((bf16[32,8,128]{2,0,1:T(8,128)(2,1)}), bf16[32,8,128]{2,0,1:T(8,128)(2,1)S(1)}, u32[]{:S(2)}, u32[]{:S(2)}) async-start(bf16[32,8,128]{2,0,1:T(8,128)(2,1)} %bitcast.5), calls=%async_computation.1 | async-start | bytes 131072 | tf_op jit(solution)/shard_map/all_to_all | solution.py:56
  26.0 44.9 %all-gather.13.cloned.1.call-start = ((), (), s32[]{:S(2)}) async-start(), calls=%async_computation.7 | async-start | bytes 2621440 | tf_op jit(solution)/shard_map/all_gather | solution.py:12
  26.8 6.9 %copy-start.39 = (pred[4,8,1]{1,0,2:T(4,128)(4,1)}, pred[4,8,1]{1,0,2:T(4,128)(4,1)S(1)}, u32[]{:S(2)}) copy-start(pred[4,8,1]{1,0,2:T(4,128)(4,1)S(1)} %fusion.83) | copy-start | bytes 100
  26.8 6.9 %copy-start.46 = (s32[1024]{0:T(1024)}, s32[1024]{0:T(1024)S(1)}, u32[]{:S(2)}) copy-start(s32[1024]{0:T(1024)S(1)} %pad_clamp_fusion) | copy-start | bytes 12292
  37.2 130.2 %all-gather.15.cloned.1.call-start = ((), (), s32[]{:S(2)}) async-start(), calls=%async_computation.8 | async-start | bytes 2621440 | tf_op jit(solution)/shard_map/all_gather | solution.py:12
  74.1 55.7 %copy-start.2 = (bf16[4,128,128]{2,1,0:T(8,128)(2,1)S(1)}, bf16[4,128,128]{2,1,0:T(8,128)(2,1)}, u32[]{:S(2)}) copy-start(bf16[4,128,128]{2,1,0:T(8,128)(2,1)} %param.12) | copy-start | bytes 393220
  74.1 55.9 %copy-start.40 = (pred[4,8,1]{1,0,2:T(4,128)(4,1)S(1)}, pred[4,8,1]{1,0,2:T(4,128)(4,1)}, u32[]{:S(2)}) copy-start(pred[4,8,1]{1,0,2:T(4,128)(4,1)} %copy-done.39) | copy-start | bytes 100
  74.1 56.1 %copy-start.1 = (f32[8,128,128]{2,1,0:T(8,128)S(1)}, f32[8,128,128]{2,1,0:T(8,128)}, u32[]{:S(2)}) copy-start(f32[8,128,128]{2,1,0:T(8,128)} %param.10) | copy-start | bytes 1572868
  74.5 58.1 %copy-start.5 = (f32[32,1024]{1,0:T(8,128)}, f32[32,1024]{1,0:T(8,128)S(1)}, u32[]{:S(2)}) copy-start(f32[32,1024]{1,0:T(8,128)S(1)} %copy.184) | copy-start | bytes 393220
  119.1 13.5 %copy-start.26 = (f32[32,8,128]{2,0,1:T(8,128)}, f32[32,8,128]{2,0,1:T(8,128)S(1)}, u32[]{:S(2)}) copy-start(f32[32,8,128]{2,0,1:T(8,128)S(1)} %get-tuple-element.51) | copy-start | bytes 393220
  132.6 132.6 %all-gather.17.cloned.1.call-start = ((), (), s32[]{:S(2)}) async-start(), calls=%async_computation.9 | async-start | bytes 2621440 | tf_op jit(solution)/shard_map/all_gather | solution.py:12
  171.4 44.9 %copy-start.27 = (f32[32,8,128]{2,0,1:T(8,128)S(1)}, f32[32,8,128]{2,0,1:T(8,128)}, u32[]{:S(2)}) copy-start(f32[32,8,128]{2,0,1:T(8,128)} %copy-done.26) | copy-start | bytes 393220
  171.4 56.4 %copy-start.41 = (pred[4,8,1]{1,0,2:T(4,128)(4,1)S(1)}, pred[4,8,1]{1,0,2:T(4,128)(4,1)}, u32[]{:S(2)}) copy-start(pred[4,8,1]{1,0,2:T(4,128)(4,1)} %copy-done.39) | copy-start | bytes 100
  172.9 57.6 %copy-start.7 = (f32[32,1024]{1,0:T(8,128)}, f32[32,1024]{1,0:T(8,128)S(1)}, u32[]{:S(2)}) copy-start(f32[32,1024]{1,0:T(8,128)S(1)} %copy.185) | copy-start | bytes 393220
  173.5 57.0 %copy-start.22 = (f32[8,32,128]{2,1,0:T(8,128)}, f32[8,32,128]{2,1,0:T(8,128)S(1)}, u32[]{:S(2)}) copy-start(f32[8,32,128]{2,1,0:T(8,128)S(1)} %fusion.46) | copy-start | bytes 393220
  217.0 13.5 %copy-start.33 = (f32[32,8,128]{2,0,1:T(8,128)}, f32[32,8,128]{2,0,1:T(8,128)S(1)}, u32[]{:S(2)}) copy-start(f32[32,8,128]{2,0,1:T(8,128)S(1)} %get-tuple-element.47) | copy-start | bytes 393220
  230.5 132.2 %all-gather.19.cloned.1.call-start = ((), (), s32[]{:S(2)}) async-start(), calls=%async_computation.10 | async-start | bytes 2621440 | tf_op jit(solution)/shard_map/all_gather | solution.py:12
  269.4 2.1 copy-start.23
  269.4 45.0 %copy-start.30 = (f32[32,8,128]{2,0,1:T(8,128)S(1)}, f32[32,8,128]{2,0,1:T(8,128)}, u32[]{:S(2)}) copy-start(f32[32,8,128]{2,0,1:T(8,128)} %get-tuple-element.48) | copy-start | bytes 393220
  269.4 45.0 %copy-start.34 = (f32[32,8,128]{2,0,1:T(8,128)S(1)}, f32[32,8,128]{2,0,1:T(8,128)}, u32[]{:S(2)}) copy-start(f32[32,8,128]{2,0,1:T(8,128)} %copy-done.33) | copy-start | bytes 393220
  269.4 55.9 %copy-start.42 = (pred[4,8,1]{1,0,2:T(4,128)(4,1)S(1)}, pred[4,8,1]{1,0,2:T(4,128)(4,1)}, u32[]{:S(2)}) copy-start(pred[4,8,1]{1,0,2:T(4,128)(4,1)} %copy-done.39) | copy-start | bytes 100
  270.8 57.0 %copy-start.9 = (f32[32,1024]{1,0:T(8,128)}, f32[32,1024]{1,0:T(8,128)S(1)}, u32[]{:S(2)}) copy-start(f32[32,1024]{1,0:T(8,128)S(1)} %copy.186) | copy-start | bytes 393220
  271.4 56.5 %copy-start.3 = (f32[8,32,128]{2,1,0:T(8,128)}, f32[8,32,128]{2,1,0:T(8,128)S(1)}, u32[]{:S(2)}) copy-start(f32[8,32,128]{2,1,0:T(8,128)S(1)} %fusion.43) | copy-start | bytes 393220
  327.9 132.3 %all-gather.21.cloned.1.call-start = ((), (), s32[]{:S(2)}) async-start(), calls=%async_computation.11 | async-start | bytes 2621440 | tf_op jit(solution)/shard_map/all_gather | solution.py:12
  366.8 2.1 copy-start.28
  366.8 45.1 %copy-start.31 = (f32[32,8,128]{2,0,1:T(8,128)S(1)}, f32[32,8,128]{2,0,1:T(8,128)}, u32[]{:S(2)}) copy-start(f32[32,8,128]{2,0,1:T(8,128)} %get-tuple-element.48) | copy-start | bytes 393220
  368.1 54.6 %copy-start.43 = (pred[4,8,1]{1,0,2:T(4,128)(4,1)S(1)}, pred[4,8,1]{1,0,2:T(4,128)(4,1)}, u32[]{:S(2)}) copy-start(pred[4,8,1]{1,0,2:T(4,128)(4,1)} %copy-done.39) | copy-start | bytes 100
  368.3 55.3 %copy-start.11 = (f32[32,1024]{1,0:T(8,128)}, f32[32,1024]{1,0:T(8,128)S(1)}, u32[]{:S(2)}) copy-start(f32[32,1024]{1,0:T(8,128)S(1)} %copy.187) | copy-start | bytes 393220
  368.9 56.6 %copy-start.20 = (f32[8,32,128]{2,1,0:T(8,128)}, f32[8,32,128]{2,1,0:T(8,128)S(1)}, u32[]{:S(2)}) copy-start(f32[8,32,128]{2,1,0:T(8,128)S(1)} %fusion.40) | copy-start | bytes 393220
  411.9 13.5 %copy-start.35 = (f32[32,8,128]{2,0,1:T(8,128)}, f32[32,8,128]{2,0,1:T(8,128)S(1)}, u32[]{:S(2)}) copy-start(f32[32,8,128]{2,0,1:T(8,128)S(1)} %get-tuple-element.40) | copy-start | bytes 393220
  425.4 132.0 %all-gather.23.cloned.1.call-start = ((), (), s32[]{:S(2)}) async-start(), calls=%async_computation.12 | async-start | bytes 2621440 | tf_op jit(solution)/shard_map/all_gather | solution.py:12
  464.3 44.8 %copy-start.36 = (f32[32,8,128]{2,0,1:T(8,128)S(1)}, f32[32,8,128]{2,0,1:T(8,128)}, u32[]{:S(2)}) copy-start(f32[32,8,128]{2,0,1:T(8,128)} %copy-done.35) | copy-start | bytes 393220
  464.3 55.7 %copy-start.44 = (pred[4,8,1]{1,0,2:T(4,128)(4,1)S(1)}, pred[4,8,1]{1,0,2:T(4,128)(4,1)}, u32[]{:S(2)}) copy-start(pred[4,8,1]{1,0,2:T(4,128)(4,1)} %copy-done.39) | copy-start | bytes 100
  465.8 56.8 %copy-start.13 = (f32[32,1024]{1,0:T(8,128)}, f32[32,1024]{1,0:T(8,128)S(1)}, u32[]{:S(2)}) copy-start(f32[32,1024]{1,0:T(8,128)S(1)} %copy.188) | copy-start | bytes 393220
  559.4 3.7 copy-start.19
  559.4 45.3 %copy-start.17 = (f32[32,1024]{1,0:T(8,128)S(1)}, f32[32,1024]{1,0:T(8,128)}, u32[]{:S(2)}) copy-start(f32[32,1024]{1,0:T(8,128)} %get-tuple-element.49) | copy-start | bytes 393220
  561.6 43.2 %copy-start.29 = (f32[32,1024]{1,0:T(8,128)S(1)}, f32[32,1024]{1,0:T(8,128)}, u32[]{:S(2)}) copy-start(f32[32,1024]{1,0:T(8,128)} %get-tuple-element.45) | copy-start | bytes 393220
  561.6 43.2 %copy-start.32 = (f32[32,1024]{1,0:T(8,128)S(1)}, f32[32,1024]{1,0:T(8,128)}, u32[]{:S(2)}) copy-start(f32[32,1024]{1,0:T(8,128)} %get-tuple-element.38) | copy-start | bytes 393220
  561.6 43.9 %copy-start.6 = (f32[32,1024]{1,0:T(8,128)S(1)}, f32[32,1024]{1,0:T(8,128)}, u32[]{:S(2)}) copy-start(f32[32,1024]{1,0:T(8,128)} %copy-done.5) | copy-start | bytes 393220
  561.6 43.9 %copy-start.8 = (f32[32,1024]{1,0:T(8,128)S(1)}, f32[32,1024]{1,0:T(8,128)}, u32[]{:S(2)}) copy-start(f32[32,1024]{1,0:T(8,128)} %copy-done.7) | copy-start | bytes 393220
  561.6 43.9 %copy-start.10 = (f32[32,1024]{1,0:T(8,128)S(1)}, f32[32,1024]{1,0:T(8,128)}, u32[]{:S(2)}) copy-start(f32[32,1024]{1,0:T(8,128)} %copy-done.9) | copy-start | bytes 393220
  561.6 43.9 %copy-start.12 = (f32[32,1024]{1,0:T(8,128)S(1)}, f32[32,1024]{1,0:T(8,128)}, u32[]{:S(2)}) copy-start(f32[32,1024]{1,0:T(8,128)} %copy-done.11) | copy-start | bytes 393220
  561.6 43.9 %copy-start.14 = (f32[32,1024]{1,0:T(8,128)S(1)}, f32[32,1024]{1,0:T(8,128)}, u32[]{:S(2)}) copy-start(f32[32,1024]{1,0:T(8,128)} %copy-done.13) | copy-start | bytes 393220
  561.6 43.9 %copy-start.25 = (f32[32,1024]{1,0:T(8,128)S(1)}, f32[32,1024]{1,0:T(8,128)}, u32[]{:S(2)}) copy-start(f32[32,1024]{1,0:T(8,128)} %param.8) | copy-start | bytes 393220
  (7 other events, 13.4 us)
Sparse Core Ops, SparseCore 0:
  37.3 33.5 all-gather.12
  132.7 34.5 all-gather.14
  230.6 34.6 all-gather.16
  328.0 34.6 all-gather.18
  425.5 34.6 all-gather.20
  522.8 34.6 all-gather.22
